TPU v7x, 32 devices: a whole 2x2x4 slice. The times are simulated.
32 devices in a mesh: grp: 2 (over y), ep: 8 (over z, x), tp: 2 (over core).
Axes of the slice: x: 2, y: 2, z: 4, core: 2. Of those that a mesh axis runs over, the one named last changes fastest.
Arguments:
- queries: bfloat16 [1024, 16, 576], P(('grp', 'ep'), 'tp'), parts along dimension 0, may hold values from -450 to 450
- latent_cache: bfloat16 [48, 512, 576], P(('grp', 'ep'), 'tp'), parts along dimension 0, may hold values from -6 to 6
- residual: bfloat16 [1024, 2048], P(('grp', 'ep')), parts along dimension 0, may hold values from -8 to 8
- token_request: int32 [1024], P(('grp', 'ep')), parts along dimension 0, may hold values from 0 to 2, as said below
- token_visible: int32 [1024], P(('grp', 'ep')), parts along dimension 0, may hold values from 1 to 512, as said below
- value_proj: bfloat16 [16, 512, 128], P('tp', 'ep'), may hold values from -0.25 to 0.25
- out_proj: bfloat16 [2048, 2048], P('tp', 'ep'), may hold values from -0.125 to 0.125
- norm_gain: float32 [2048], replicated, may hold values from 0.1 to 1.9
- router: bfloat16 [2048, 64], replicated, may hold values from -0.0390625 to 0.0390625
- expert_ids: int32 [1024, 6], P(('grp', 'ep')), parts along dimension 0, may hold values from 0 to 63, all different within a row; in each aligned block of 64 rows (0 to 63, 64 to 127, ...) at most 8 rows name the same one
- gate_weight: bfloat16 [128, 2048, 384], P('ep', None, 'tp'), may hold values from -0.125 to 0.125
- up_weight: bfloat16 [128, 2048, 384], P('ep', None, 'tp'), may hold values from -0.125 to 0.125
- down_weight: bfloat16 [128, 384, 2048], P('ep', 'tp'), may hold values from -0.21875 to 0.21875
Outputs:
- hidden: bfloat16 [1024, 2048], P(('grp', 'ep'), 'tp'), parts along dimension 0
- expert_out: bfloat16 [1024, 2048], P(('grp', 'ep'), 'tp'), parts along dimension 0
There are 2 independent parts, one for each index of `grp`. A program takes and returns all parts, laid end to end along the dimension named above; an argument that names none is the same for every part. Nothing has to cross between parts.
Inputs may be any that keep to these rules, and one draw needn't show every extreme that they name: `token_request`: in each ep block, 62 tokens belong to request 0, a prefill span, and each other request has exactly one token; the tokens' order in the block is arbitrary. `token_visible`: the span's tokens read consecutive counts s + 1 to s + 62; 512 is reached in every draw. `expert_ids`: each row names 6 different experts; among the 64 tokens of one ep index no expert is named by more than 8 tokens, and this bound is reached.
All inputs are finite; a program needn't handle non-finite values.
Results may differ from a plain program's by a relative error of at most 0.018.
Values may be sent and summed in bfloat16 or wider, within the bound.
A program may use at most 128 MiB of HBM per device.

v0:
```python
import jax
import jax.numpy as jnp
from jax import lax
from jax.sharding import PartitionSpec as P

LATENT = 512
VDIM = 128
EXPERTS = 64
TOPK = 6
GROUPS = 2
CAP = 8
PIECES = 128
score_scale = 192.0 ** (-0.5)
epsilon = 1e-06


def masked_scores(queries, block_rows, token_request, token_visible):
    per_request = block_rows.shape[1]
    flat_rows = block_rows.reshape(-1, block_rows.shape[2])
    scores = (
        jnp.einsum("thc,kc->thk", queries, flat_rows, preferred_element_type=jnp.float32)
        * score_scale
    )
    column = jnp.arange(flat_rows.shape[0], dtype=jnp.int32)
    owner_id = column // per_request
    position = column % per_request
    allowed = (owner_id[None, :] == token_request[:, None]) & (
        position[None, :] < token_visible[:, None]
    )
    return (jnp.where(allowed[:, None, :], scores, -jnp.inf), flat_rows)


def weighted_rows(scores, row_peak, flat_rows):
    weights = jnp.exp(scores - row_peak[:, :, None]).astype(jnp.bfloat16)
    totals = jnp.sum(weights.astype(jnp.float32), axis=2)
    summed = jnp.einsum(
        "thk,kc->thc", weights, flat_rows[:, :LATENT], preferred_element_type=jnp.float32
    )
    return (summed, totals)


def expert_block(arrived, gate_weight, up_weight, down_weight):
    gate_vals = jnp.einsum("prd,pdf->prf", arrived, gate_weight, preferred_element_type=jnp.float32)
    up_vals = jnp.einsum("prd,pdf->prf", arrived, up_weight, preferred_element_type=jnp.float32)
    activated = (jax.nn.silu(gate_vals) * up_vals).astype(jnp.bfloat16)
    return jnp.einsum(
        "prf,pfd->prd", activated, down_weight, preferred_element_type=jnp.float32
    ).astype(jnp.bfloat16)


def body(
    queries,
    latent_cache,
    residual,
    token_request,
    token_visible,
    value_proj,
    out_proj,
    norm_gain,
    router,
    expert_ids,
    gate_weight,
    up_weight,
    down_weight,
):
    all_rows = lax.all_gather(latent_cache, "tp", axis=1, tiled=True)
    scores, flat_rows = masked_scores(queries, all_rows, token_request, token_visible)
    summed, totals = weighted_rows(scores, jnp.max(scores, axis=2), flat_rows)
    context = (summed / totals[:, :, None]).astype(jnp.bfloat16)
    tokens_here = context.shape[0]
    heads_here = context.shape[1]
    head_values = jnp.einsum(
        "thl,hlv->thv",
        context,
        lax.all_gather(value_proj, "ep", axis=1, tiled=True),
        preferred_element_type=jnp.float32,
    )
    heads_out = head_values.astype(jnp.bfloat16).reshape(tokens_here, heads_here * VDIM)
    column_block = jnp.dot(
        lax.all_gather(heads_out, "ep", axis=0, tiled=True),
        out_proj,
        preferred_element_type=jnp.float32,
    )
    attention_part = lax.all_to_all(column_block, "ep", split_axis=0, concat_axis=1, tiled=True)
    attention = lax.psum(attention_part, "tp")
    hidden = (residual.astype(jnp.float32) + attention).astype(jnp.bfloat16)
    hidden_wide = hidden.astype(jnp.float32)
    normed = (
        hidden_wide
        * lax.rsqrt(jnp.mean(hidden_wide * hidden_wide, axis=1, keepdims=True) + epsilon)
        * norm_gain
    ).astype(jnp.bfloat16)
    logits = jnp.dot(normed, router, preferred_element_type=jnp.float32)
    gate_share = jax.nn.softmax(jnp.take_along_axis(logits, expert_ids, axis=1), axis=1).astype(
        jnp.bfloat16
    )
    flat_ids = expert_ids.reshape(-1)
    position_id = jnp.arange(flat_ids.shape[0], dtype=jnp.int32)
    earlier = (flat_ids[:, None] == flat_ids[None, :]) & (
        position_id[None, :] < position_id[:, None]
    )
    slot_ids = (flat_ids * CAP + jnp.sum(earlier.astype(jnp.int32), axis=1)).reshape(
        tokens_here, TOPK
    )
    targets = jnp.arange(EXPERTS * CAP, dtype=jnp.int32)
    matches = slot_ids[:, :, None] == targets[None, None, :]
    picker = jnp.any(matches, axis=1).T.astype(jnp.bfloat16)
    model_width = normed.shape[1]
    mixing = jnp.sum(
        jnp.where(matches, gate_share[:, :, None], jnp.zeros((), jnp.bfloat16)), axis=1
    )
    mixing = jnp.broadcast_to(
        mixing.reshape(tokens_here, EXPERTS, 1, CAP), (tokens_here, EXPERTS, GROUPS, CAP)
    ).reshape(tokens_here, PIECES * CAP)
    core_count = lax.axis_size("tp")
    half_width = model_width // core_count
    core_start = lax.axis_index("tp") * half_width
    outgoing = jnp.dot(picker, normed, preferred_element_type=jnp.float32).astype(jnp.bfloat16)
    outgoing = jnp.broadcast_to(
        outgoing.reshape(EXPERTS, 1, CAP, model_width), (EXPERTS, GROUPS, CAP, model_width)
    ).reshape(PIECES, CAP, model_width)
    arrived = lax.all_to_all(outgoing, "ep", split_axis=0, concat_axis=1, tiled=True)
    partial_out = expert_block(arrived, gate_weight, up_weight, down_weight)
    returned = lax.all_to_all(partial_out, "ep", split_axis=1, concat_axis=0, tiled=True)
    routed = jnp.dot(
        mixing, returned.reshape(PIECES * CAP, model_width), preferred_element_type=jnp.float32
    )
    expert_out = lax.psum_scatter(
        routed.astype(jnp.bfloat16), "tp", scatter_dimension=1, tiled=True
    )
    hidden_part = lax.dynamic_slice_in_dim(hidden, core_start, half_width, 1)
    return (hidden_part, expert_out)


def solution(mesh):
    return jax.shard_map(
        body,
        mesh=mesh,
        in_specs=(
            P(("grp", "ep"), "tp", None),
            P(("grp", "ep"), "tp", None),
            P(("grp", "ep"), None),
            P(("grp", "ep")),
            P(("grp", "ep")),
            P("tp", "ep", None),
            P("tp", "ep"),
            P(),
            P(),
            P(("grp", "ep"), None),
            P("ep", None, "tp"),
            P("ep", None, "tp"),
            P("ep", "tp", None),
        ),
        out_specs=(P(("grp", "ep"), "tp"), P(("grp", "ep"), "tp")),
        check_vma=False,
    )
```

profile of v0, /device:TPU:0, one launch (start us, length us, event | category | flops | bytes accessed | tf_op | source)
XLA Modules:
  0.0 395.9 jit_solution(957612986233958496)
XLA Ops:
  8.7 0.8 compare_and_fusion
  9.6 12.4 %all-gather.4.cloned.1.call-done = bf16[3,512,576]{1,2,0:T(8,128)(2,1)} async-done(((bf16[3,256,576]{1,2,0:T(8,128)(2,1)}), bf16[3,512,576]{1,2,0:T(8,128)(2,1)}) %all-gather.4.cloned.1.call-update) | async-done | bytes 1769488 | tf_op jit(solution)/shard_map/all_gather | solution.py:66
  22.0 2.7 copy.88
  24.7 3.2 convert_reduce_fusion
  28.0 37.6 %all-gather.6.cloned.1.call-done = bf16[8,512,128]{2,1,0:T(8,128)(2,1)} async-done(((bf16[8,64,128]{2,1,0:T(8,128)(2,1)}), bf16[8,512,128]{2,1,0:T(8,128)(2,1)}) %all-gather.6.cloned.1.call-update) | async-done | bytes 1048592 | tf_op jit(solution)/shard_map/all_gather | solution.py:75
  65.6 2.9 fusion.22
  69.3 39.1 %all-gather.8.cloned.1.call-done = bf16[512,1024]{1,0:T(8,128)(2,1)} async-done(((bf16[64,1024]{1,0:T(8,128)(2,1)}), bf16[512,1024]{1,0:T(8,128)(2,1)}) %all-gather.8.cloned.1.call-update) | async-done | bytes 1048592 | tf_op jit(solution)/shard_map/all_gather | solution.py:80
  108.4 1.7 fusion.54
  110.1 15.7 %all_to_all.52 = f32[8,64,256]{2,1,0:T(8,128)S(1)} all-to-all(f32[8,64,256]{2,1,0:T(8,128)S(1)} %bitcast.65), channel_id=1, replica_groups=mesh['grp'=2,'ep'=8,'tp'=2] {'ep'}, dimensions={0} | all-to-all | bytes 1048576 | tf_op jit(solution)/shard_map/all_to_all | solution.py:84
  125.8 0.9 copy.107
  127.6 16.9 %all-reduce.2.cloned.1.call-done = f32[64,2048]{1,0:T(8,128)} async-done(((f32[64,2048]{1,0:T(8,128)}), f32[64,2048]{1,0:T(8,128)}) %all-reduce.2.cloned.1.call-update) | async-done | bytes 524304 | tf_op jit(solution)/shard_map/psum | solution.py:85
  144.5 1.2 fusion.35
  145.8 0.8 fusion.11
  147.1 99.2 %all_to_all.53 = bf16[128,8,2048]{2,1,0:T(8,128)(2,1)S(1)} all-to-all(bf16[128,8,2048]{2,1,0:T(8,128)(2,1)S(1)} %bitcast.62), channel_id=1, replica_groups=mesh['grp'=2,'ep'=8,'tp'=2] {'ep'}, dimensions={0} | all-to-all | bytes 8388608 | tf_op jit(solution)/shard_map/all_to_all | solution.py:122
  246.3 2.0 copy-done.2
  248.3 10.0 %fusion.3 = f32[16,64,192]{2,1,0:T(8,128)} fusion(bf16[16,2048,192]{1,2,0:T(8,128)(2,1)} %param.23, bf16[16,8,8,2048]{3,2,0,1:T(8,128)(2,1)S(1)} %bitcast.59), kind=kOutput, calls=%fused_computation.4 | convolution fusion | flops 805306368 | bytes 17563648 | tf_op jit(solution)/shard_map/prd,pdf->prf/dot_general | solution.py:43
  258.2 14.3 %convolution_convert_fusion = bf16[16,64,2048]{2,1,0:T(8,128)(2,1)} fusion(bf16[16,192,2048]{2,1,0:T(8,128)(2,1)} %param.25, bf16[16,2048,192]{1,2,0:T(8,128)(2,1)} %param.24, bf16[16,8,8,2048]{3,2,0,1:T(8,128)(2,1)} %bitcast.60, f32[16,64,192]{2,1,0:T(8,128)} %fusion.3), kind=kOutput, calls=%fused_computation.7 | convolution fusion | flops 1613889536 | bytes 34340864 | tf_op jit(solution)/shard_map/prf,pfd->prd/dot_general | solution.py:46
  272.5 6.5 %copy.100 = bf16[16,64,2048]{2,0,1:T(8,128)(2,1)} copy(bf16[16,64,2048]{2,1,0:T(8,128)(2,1)} %convolution_convert_fusion) | data formatting | bytes 8388608 | tf_op jit(solution)/shard_map/convert_element_type | solution.py:48
  279.0 4.7 %all-to-all-start.2 = ((bf16[16,64,2048]{2,0,1:T(8,128)(2,1)}), bf16[16,64,2048]{2,0,1:T(8,128)(2,1)}, u32[]{:S(2)}, u32[]{:S(2)}) async-start(bf16[16,64,2048]{2,0,1:T(8,128)(2,1)} %copy.100), calls=%async_computation.2 | async-start | bytes 8388608 | tf_op jit(solution)/shard_map/all_to_all | solution.py:124
  284.5 2.9 gather_fusion
  288.0 88.1 %all-to-all-done.2 = bf16[16,64,2048]{2,0,1:T(8,128)(2,1)} async-done(((bf16[16,64,2048]{2,0,1:T(8,128)(2,1)}), bf16[16,64,2048]{2,0,1:T(8,128)(2,1)}, u32[]{:S(2)}, u32[]{:S(2)}) %all-to-all-start.2) | async-done | bytes 4194336 | tf_op jit(solution)/shard_map/all_to_all | solution.py:124
  376.1 4.7 %copy.102 = bf16[8,16,8,2048]{3,2,1,0:T(8,128)(2,1)S(1)} copy(bf16[8,16,8,2048]{3,1,2,0:T(8,128)(2,1)} %bitcast.16) | data formatting | bytes 8388608 | tf_op jit(solution)/shard_map/all_to_all | solution.py:124
  380.8 1.6 convolution_convert_fusion.2
  383.1 6.2 %reduce-scatter.2.cloned.1.call-done = bf16[64,1024]{1,0:T(8,128)(2,1)} async-done(((bf16[64,2048]{1,0:T(8,128)(2,1)}), bf16[64,1024]{1,0:T(8,128)(2,1)}) %reduce-scatter.2.cloned.1.call-update) | async-done | bytes 131088 | tf_op jit(solution)/shard_map/reduce_scatter | solution.py:128
  (50 shorter events, 5.9 us)
Async XLA Ops:
  7.2 17.6 %copy-start = (bf16[64,8,576]{2,1,0:T(8,128)(2,1)S(1)}, bf16[64,8,576]{2,1,0:T(8,128)(2,1)}, u32[]{:S(2)}) copy-start(bf16[64,8,576]{2,1,0:T(8,128)(2,1)} %param.13) | copy-start | bytes 1769476
  7.2 14.8 %all-gather.4.cloned.1.call-start = ((), (), s32[]{:S(2)}) async-start(), calls=%async_computation.4 | async-start | bytes 2654208 | tf_op jit(solution)/shard_map/all_gather | solution.py:66
  7.9 57.7 %all-gather.6.cloned.1.call-start = ((), (), s32[]{:S(2)}) async-start(), calls=%async_computation.5 | async-start | bytes 1179648 | tf_op jit(solution)/shard_map/all_gather | solution.py:75
  8.7 99.8 %all-gather.8.cloned.1.call-start = ((), (), s32[]{:S(2)}) async-start(), calls=%async_computation.6 | async-start | bytes 1179648 | tf_op jit(solution)/shard_map/all_gather | solution.py:80
  65.6 42.8 %copy-start.3 = (bf16[1024,256]{1,0:T(8,128)(2,1)S(1)}, bf16[1024,256]{1,0:T(8,128)(2,1)}, u32[]{:S(2)}) copy-start(bf16[1024,256]{1,0:T(8,128)(2,1)} %param.19) | copy-start | bytes 1572868
  68.5 58.2 %copy-start.5 = (s32[64,6]{0,1:T(8,128)S(1)}, s32[64,6]{0,1:T(8,128)}, u32[]{:S(2)}) copy-start(s32[64,6]{0,1:T(8,128)} %param.22) | copy-start | bytes 4612
  68.6 76.0 %copy-start.4 = (bf16[64,2048]{1,0:T(8,128)(2,1)S(1)}, bf16[64,2048]{1,0:T(8,128)(2,1)}, u32[]{:S(2)}) copy-start(bf16[64,2048]{1,0:T(8,128)(2,1)} %param.15) | copy-start | bytes 786436
  68.6 77.2 %copy-start.6 = (f32[2048]{0:T(1024)S(1)}, f32[2048]{0:T(1024)}, u32[]{:S(2)}) copy-start(f32[2048]{0:T(1024)} %param.20) | copy-start | bytes 24580
  69.3 75.2 %all-reduce.2.cloned.1.call-start = ((), (), s32[]{:S(2)}) async-start(), calls=%async_computation.7 | async-start | bytes 1048576 | tf_op jit(solution)/shard_map/psum | solution.py:85
  246.3 2.0 copy-start.2
  279.0 5.2 %copy-start.7 = (bf16[2048,64]{0,1:T(8,128)(2,1)S(1)}, bf16[2048,64]{0,1:T(8,128)(2,1)}, u32[]{:S(2)}) copy-start(bf16[2048,64]{0,1:T(8,128)(2,1)} %param.21) | copy-start | bytes 786436
  279.0 97.1 %all-to-all-start.2 = ((bf16[16,64,2048]{2,0,1:T(8,128)(2,1)}), bf16[16,64,2048]{2,0,1:T(8,128)(2,1)}, u32[]{:S(2)}, u32[]{:S(2)}) async-start(bf16[16,64,2048]{2,0,1:T(8,128)(2,1)} %copy.100), calls=%async_computation.2 | async-start | bytes 8388608 | tf_op jit(solution)/shard_map/all_to_all | solution.py:124
  283.7 105.7 %reduce-scatter.2.cloned.1.call-start = ((), (), s32[]{:S(2)}) async-start(), calls=%async_computation.8 | async-start | bytes 393216 | tf_op jit(solution)/shard_map/reduce_scatter | solution.py:128
  376.1 13.2 %copy-start.1 = (bf16[64,8,576]{2,1,0:T(8,128)(2,1)S(1)}, bf16[64,8,576]{2,1,0:T(8,128)(2,1)}, u32[]{:S(2)}) copy-start(bf16[64,8,576]{2,1,0:T(8,128)(2,1)} %param.13) | copy-start | bytes 1769476
Sparse Core Ops, SparseCore 0:
  9.5 12.4 all-gather.3
  24.2 41.4 all-gather.5
  69.4 38.9 all-gather.7
  126.8 17.6 all-reduce.1
  382.5 6.7 reduce-scatter.1
where the time goes:
time: 396 us
  waiting for transfers between devices  202 us (51%)
  blocking collectives  115 us (29%)
  matrix products  34.7 us (9%)
  local copies, waits for them, and re-layouts  22.6 us (6%)
  between operations  14 us (4%)
  starting transfers between devices  5.09 us (1%)
    all_to_all x1, blocking collectives, body(): lax.all_to_all(outgoing, 'ep', split_axis=0, concat_axis=1, tiled=True)  99.2 us
    all_to_all x1, waiting for transfers between devices, body(): lax.all_to_all(partial_out, 'ep', split_axis=1, concat_axis=0, tiled=True)  88.1 us
    all_gather x1, waiting for transfers between devices, body(): lax.all_gather(heads_out, 'ep', axis=0, tiled=True)  39.1 us
    all_gather x1, waiting for transfers between devices, body(): lax.all_gather(value_proj, 'ep', axis=1, tiled=True)  37.6 us
    psum x1, waiting for transfers between devices, body(): attention = lax.psum(attention_part, 'tp')  16.9 us
    all_to_all x1, blocking collectives, body(): lax.all_to_all(column_block, 'ep', split_axis=0, concat_axis=1, tiled=True)  15.7 us
    dot_general x1, matrix products, expert_block(): jnp.einsum('prf,pfd->prd', activated, down_weight, preferred_element_type...  14.3 us
    all_gather x1, waiting for transfers between devices, body(): all_rows = lax.all_gather(latent_cache, 'tp', axis=1, tiled=True)  12.4 us
  transfers between devices with their start and end apart: 6, of which 6 were waited for; matrix products, arithmetic and copies ran while one was open for 3% of the time, Pallas kernels for 0%

commit v1 on v0

--- a/solution.py
+++ b/solution.py
@@ -12,6 +12,22 @@
 PIECES = 128
 score_scale = 192.0 ** (-0.5)
 epsilon = 1e-06
+
+
+def product_in_turn(x, axis, dim, term):
+    size, index, rows = (lax.axis_size(axis), lax.axis_index(axis), x.shape[dim])
+    ahead = [(i, (i + 1) % size) for i in range(size)]
+    left = [(i, (i - 1) % size) for i in range(size)]
+    half = size // 2
+    from_left = from_right = x
+    total = term(x, index * rows)
+    for hop in range(1, half + 1):
+        from_left = lax.ppermute(from_left, axis, ahead)
+        if hop < size - half:
+            from_right = lax.ppermute(from_right, axis, left)
+            total = total + term(from_right, (index + hop) % size * rows)
+        total = total + term(from_left, (index - hop) % size * rows)
+    return total
 
 
 def masked_scores(queries, block_rows, token_request, token_visible):
@@ -69,11 +85,16 @@
     context = (summed / totals[:, :, None]).astype(jnp.bfloat16)
     tokens_here = context.shape[0]
     heads_here = context.shape[1]
-    head_values = jnp.einsum(
-        "thl,hlv->thv",
-        context,
-        lax.all_gather(value_proj, "ep", axis=1, tiled=True),
-        preferred_element_type=jnp.float32,
+    head_values = product_in_turn(
+        value_proj,
+        "ep",
+        1,
+        lambda shard, start: jnp.einsum(
+            "thl,hlv->thv",
+            lax.dynamic_slice_in_dim(context, start, shard.shape[1], axis=2),
+            shard,
+            preferred_element_type=jnp.float32,
+        ),
     )
     heads_out = head_values.astype(jnp.bfloat16).reshape(tokens_here, heads_here * VDIM)
     column_block = jnp.dot(

time: 396 us -> 376 us (0.949)
  waiting for transfers between devices: 202 us -> 162 us
  starting transfers between devices: 5.09 us -> 21.7 us
    all_gather x1 -> x0, waiting for transfers between devices: 37.6 us -> none  [body(): lax.all_gather(value_proj, 'ep', axis=1, tiled=True)]
    ppermute x0 -> x7, starting transfers between devices: none -> 16.7 us  [the longest x3 9.74 us: product_in_turn(): from_right = lax.ppermute(from_right, axis, left)]
    all_gather x1, waiting for transfers between devices: 12.4 us -> 0.01 us  [body(): all_rows = lax.all_gather(latent_cache, 'tp', axis=1, tiled=True)]
    ppermute x0 -> x7, waiting for transfers between devices: none -> 8.5 us  [the longest x4 8.49 us: product_in_turn(): from_left = lax.ppermute(from_left, axis, ahead)]
  transfers between devices with their start and end apart: 6 -> 12, of which waited for: 6 -> 7; matrix products, arithmetic and copies ran while one was open for 3% -> 5% of each run, Pallas kernels for 0% -> 0%
where the time goes in v1:
time: 376 us; the launch traced here: 375 us
  waiting for transfers between devices  162 us (43%)
  blocking collectives  115 us (31%)
  matrix products  36.5 us (10%)
  local copies, waits for them, and re-layouts  22.9 us (6%)
  starting transfers between devices  21.7 us (6%)
  between operations  14.2 us (4%)
    all_to_all x1, blocking collectives, body(): lax.all_to_all(outgoing, 'ep', split_axis=0, concat_axis=1, tiled=True)  99.2 us
    all_to_all x1, waiting for transfers between devices, body(): lax.all_to_all(partial_out, 'ep', split_axis=1, concat_axis=0, tiled=True)  88.1 us
    all_gather x1, waiting for transfers between devices, body(): lax.all_gather(heads_out, 'ep', axis=0, tiled=True)  41.6 us
    psum x1, waiting for transfers between devices, body(): attention = lax.psum(attention_part, 'tp')  16.9 us
    all_to_all x1, blocking collectives, body(): lax.all_to_all(column_block, 'ep', split_axis=0, concat_axis=1, tiled=True)  15.7 us
    dot_general x1, matrix products, expert_block(): jnp.einsum('prf,pfd->prd', activated, down_weight, preferred_element_type...  14.3 us
    dot_general x1, matrix products, expert_block(): jnp.einsum('prd,pdf->prf', arrived, gate_weight, preferred_element_type=j...  9.93 us
    ppermute x3, starting transfers between devices, product_in_turn(): from_right = lax.ppermute(from_right, axis, left)  9.74 us
  transfers between devices with their start and end apart: 12, of which 7 were waited for; matrix products, arithmetic and copies ran while one was open for 5% of the time, Pallas kernels for 0%

profile of v1, /device:TPU:0, one launch (start us, length us, event | category | flops | bytes accessed | tf_op | source)
XLA Modules:
  0.0 375.0 jit_solution(8934345797703294140)
XLA Ops:
  8.0 3.0 collective-permute-start.1
  11.0 3.1 collective-permute-start
  14.1 3.7 collective-permute-done.1
  19.2 3.5 collective-permute-start.2
  22.8 2.7 collective-permute-done.3
  25.5 1.7 collective-permute-start.5
  28.1 3.1 collective-permute-start.4
  31.2 2.0 collective-permute-done.5
  34.1 2.7 copy.123
  36.8 3.2 convert_reduce_fusion
  40.1 2.4 fusion.23
  46.0 41.6 %all-gather.5.cloned.1.call-done = bf16[512,1024]{1,0:T(8,128)(2,1)} async-done(((bf16[64,1024]{1,0:T(8,128)(2,1)}), bf16[512,1024]{1,0:T(8,128)(2,1)}) %all-gather.5.cloned.1.call-update) | async-done | bytes 1048592 | tf_op jit(solution)/shard_map/all_gather | solution.py:101
  89.3 15.7 %all_to_all.52 = f32[8,64,256]{2,1,0:T(8,128)S(1)} all-to-all(f32[8,64,256]{2,1,0:T(8,128)S(1)} %bitcast.73), channel_id=1, replica_groups=mesh['grp'=2,'ep'=8,'tp'=2] {'ep'}, dimensions={0} | all-to-all | bytes 1048576 | tf_op jit(solution)/shard_map/all_to_all | solution.py:105
  106.8 16.9 %all-reduce.2.cloned.1.call-done = f32[64,2048]{1,0:T(8,128)} async-done(((f32[64,2048]{1,0:T(8,128)}), f32[64,2048]{1,0:T(8,128)}) %all-reduce.2.cloned.1.call-update) | async-done | bytes 524304 | tf_op jit(solution)/shard_map/psum | solution.py:106
  126.2 99.2 %all_to_all.53 = bf16[128,8,2048]{2,1,0:T(8,128)(2,1)S(1)} all-to-all(bf16[128,8,2048]{2,1,0:T(8,128)(2,1)S(1)} %bitcast.70), channel_id=1, replica_groups=mesh['grp'=2,'ep'=8,'tp'=2] {'ep'}, dimensions={0} | all-to-all | bytes 8388608 | tf_op jit(solution)/shard_map/all_to_all | solution.py:143
  225.4 2.0 copy-done.2
  227.4 9.9 %fusion.2 = f32[16,64,192]{2,1,0:T(8,128)} fusion(bf16[16,2048,192]{1,2,0:T(8,128)(2,1)} %param.23, bf16[16,8,8,2048]{3,2,0,1:T(8,128)(2,1)S(1)} %bitcast.67), kind=kOutput, calls=%fused_computation.3 | convolution fusion | flops 805306368 | bytes 17563648 | tf_op jit(solution)/shard_map/prd,pdf->prf/dot_general | solution.py:59
  237.3 14.3 %convolution_convert_fusion = bf16[16,64,2048]{2,1,0:T(8,128)(2,1)} fusion(bf16[16,192,2048]{2,1,0:T(8,128)(2,1)} %param.25, bf16[16,2048,192]{1,2,0:T(8,128)(2,1)} %param.24, bf16[16,8,8,2048]{3,2,0,1:T(8,128)(2,1)} %bitcast.68, f32[16,64,192]{2,1,0:T(8,128)} %fusion.2), kind=kOutput, calls=%fused_computation.5 | convolution fusion | flops 1613889536 | bytes 34340864 | tf_op jit(solution)/shard_map/prf,pfd->prd/dot_general | solution.py:62
  251.6 6.4 %copy.141 = bf16[16,64,2048]{2,0,1:T(8,128)(2,1)} copy(bf16[16,64,2048]{2,1,0:T(8,128)(2,1)} %convolution_convert_fusion) | data formatting | bytes 8388608 | tf_op jit(solution)/shard_map/convert_element_type | solution.py:64
  258.1 4.7 %all-to-all-start.2 = ((bf16[16,64,2048]{2,0,1:T(8,128)(2,1)}), bf16[16,64,2048]{2,0,1:T(8,128)(2,1)}, u32[]{:S(2)}, u32[]{:S(2)}) async-start(bf16[16,64,2048]{2,0,1:T(8,128)(2,1)} %copy.141), calls=%async_computation.2 | async-start | bytes 8388608 | tf_op jit(solution)/shard_map/all_to_all | solution.py:145
  263.6 2.9 gather_fusion
  267.1 88.1 %all-to-all-done.2 = bf16[16,64,2048]{2,0,1:T(8,128)(2,1)} async-done(((bf16[16,64,2048]{2,0,1:T(8,128)(2,1)}), bf16[16,64,2048]{2,0,1:T(8,128)(2,1)}, u32[]{:S(2)}, u32[]{:S(2)}) %all-to-all-start.2) | async-done | bytes 4194336 | tf_op jit(solution)/shard_map/all_to_all | solution.py:145
  355.2 4.7 %copy.143 = bf16[8,16,8,2048]{3,2,1,0:T(8,128)(2,1)S(1)} copy(bf16[8,16,8,2048]{3,1,2,0:T(8,128)(2,1)} %bitcast.16) | data formatting | bytes 8388608 | tf_op jit(solution)/shard_map/all_to_all | solution.py:145
  362.2 6.2 %reduce-scatter.2.cloned.1.call-done = bf16[64,1024]{1,0:T(8,128)(2,1)} async-done(((bf16[64,2048]{1,0:T(8,128)(2,1)}), bf16[64,1024]{1,0:T(8,128)(2,1)}) %reduce-scatter.2.cloned.1.call-update) | async-done | bytes 131088 | tf_op jit(solution)/shard_map/reduce_scatter | solution.py:149
  (71 shorter events, 16.8 us)
Async XLA Ops:
  7.2 29.7 %copy-start = (bf16[64,8,576]{2,1,0:T(8,128)(2,1)S(1)}, bf16[64,8,576]{2,1,0:T(8,128)(2,1)}, u32[]{:S(2)}) copy-start(bf16[64,8,576]{2,1,0:T(8,128)(2,1)} %param.13) | copy-start | bytes 1769476
  7.2 26.9 %all-gather.3.cloned.1.call-start = ((), (), s32[]{:S(2)}) async-start(), calls=%async_computation.4 | async-start | bytes 2654208 | tf_op jit(solution)/shard_map/all_gather | solution.py:82
  7.9 79.7 %all-gather.5.cloned.1.call-start = ((), (), s32[]{:S(2)}) async-start(), calls=%async_computation.5 | async-start | bytes 1179648 | tf_op jit(solution)/shard_map/all_gather | solution.py:101
  8.0 9.9 %collective-permute-start.1 = (bf16[8,64,128]{2,1,0:T(8,128)(2,1)}, bf16[8,64,128]{2,1,0:T(8,128)(2,1)S(1)}, u32[]{:S(2)}, u32[]{:S(2)}) collective-permute-start(bf16[8,64,128]{2,1,0:T(8,128)(2,1)} %param.18), channel_id=1, source_target_pairs={{0,2},{2,4},{4,6},{6,8},{8,10},{10,12},{12,14},{14,0},{1,3},{3,5},... | collective-permute-start | bytes 393224 | tf_op jit(solution)/shard_map/ppermute | solution.py:25
  11.0 8.3 %collective-permute-start = (bf16[8,64,128]{2,1,0:T(8,128)(2,1)}, bf16[8,64,128]{2,1,0:T(8,128)(2,1)S(1)}, u32[]{:S(2)}, u32[]{:S(2)}) collective-permute-start(bf16[8,64,128]{2,1,0:T(8,128)(2,1)} %param.18), channel_id=1, source_target_pairs={{0,14},{2,0},{4,2},{6,4},{8,6},{10,8},{12,10},{14,12},{1,15},{3,1}... | collective-permute-start | bytes 393224 | tf_op jit(solution)/shard_map/ppermute | solution.py:27
  17.8 7.7 %collective-permute-start.3 = (bf16[8,64,128]{2,1,0:T(8,128)(2,1)S(1)}, bf16[8,64,128]{2,1,0:T(8,128)(2,1)S(1)}, u32[]{:S(2)}, u32[]{:S(2)}) collective-permute-start(bf16[8,64,128]{2,1,0:T(8,128)(2,1)S(1)} %collective-permute-done.1), channel_id=1, source_target_pairs={{0,2},{2,4},{4,6},{6,8},{8,10},{10,12},{12,14},{14,0},{1,3},{3,5},... | collective-permute-start | bytes 393224 | tf_op jit(solution)/shard_map/ppermute | solution.py:25
  19.2 8.9 %collective-permute-start.2 = (bf16[8,64,128]{2,1,0:T(8,128)(2,1)S(1)}, bf16[8,64,128]{2,1,0:T(8,128)(2,1)S(1)}, u32[]{:S(2)}, u32[]{:S(2)}) collective-permute-start(bf16[8,64,128]{2,1,0:T(8,128)(2,1)S(1)} %collective-permute-done), channel_id=1, source_target_pairs={{0,14},{2,0},{4,2},{6,4},{8,6},{10,8},{12,10},{14,12},{1,15},{3,1}... | collective-permute-start | bytes 393224 | tf_op jit(solution)/shard_map/ppermute | solution.py:27
  25.5 7.8 %collective-permute-start.5 = (bf16[8,64,128]{2,1,0:T(8,128)(2,1)S(1)}, bf16[8,64,128]{2,1,0:T(8,128)(2,1)S(1)}, u32[]{:S(2)}, u32[]{:S(2)}) collective-permute-start(bf16[8,64,128]{2,1,0:T(8,128)(2,1)S(1)} %collective-permute-done.3), channel_id=1, source_target_pairs={{0,2},{2,4},{4,6},{6,8},{8,10},{10,12},{12,14},{14,0},{1,3},{3,5},... | collective-permute-start | bytes 393224 | tf_op jit(solution)/shard_map/ppermute | solution.py:25
  28.1 15.9 %collective-permute-start.4 = (bf16[8,64,128]{2,1,0:T(8,128)(2,1)S(1)}, bf16[8,64,128]{2,1,0:T(8,128)(2,1)}, u32[]{:S(2)}, u32[]{:S(2)}) collective-permute-start(bf16[8,64,128]{2,1,0:T(8,128)(2,1)S(1)} %collective-permute-done.2), channel_id=1, source_target_pairs={{0,14},{2,0},{4,2},{6,4},{8,6},{10,8},{12,10},{14,12},{1,15},{3,1}... | collective-permute-start | bytes 393224 | tf_op jit(solution)/shard_map/ppermute | solution.py:27
  33.3 11.8 %collective-permute-start.6 = (bf16[8,64,128]{2,1,0:T(8,128)(2,1)S(1)}, bf16[8,64,128]{2,1,0:T(8,128)(2,1)S(1)}, u32[]{:S(2)}, u32[]{:S(2)}) collective-permute-start(bf16[8,64,128]{2,1,0:T(8,128)(2,1)S(1)} %collective-permute-done.5), channel_id=1, source_target_pairs={{0,2},{2,4},{4,6},{6,8},{8,10},{10,12},{12,14},{14,0},{1,3},{3,5},... | collective-permute-start | bytes 393224 | tf_op jit(solution)/shard_map/ppermute | solution.py:25
  40.1 2.8 copy-start.6
  42.5 45.1 %copy-start.3 = (bf16[1024,256]{1,0:T(8,128)(2,1)S(1)}, bf16[1024,256]{1,0:T(8,128)(2,1)}, u32[]{:S(2)}) copy-start(bf16[1024,256]{1,0:T(8,128)(2,1)} %param.19) | copy-start | bytes 1572868
  43.6 62.3 %copy-start.5 = (s32[64,6]{0,1:T(8,128)S(1)}, s32[64,6]{0,1:T(8,128)}, u32[]{:S(2)}) copy-start(s32[64,6]{0,1:T(8,128)} %param.22) | copy-start | bytes 4612
  43.6 80.0 %copy-start.4 = (bf16[64,2048]{1,0:T(8,128)(2,1)S(1)}, bf16[64,2048]{1,0:T(8,128)(2,1)}, u32[]{:S(2)}) copy-start(bf16[64,2048]{1,0:T(8,128)(2,1)} %param.15) | copy-start | bytes 786436
  43.8 81.1 %copy-start.7 = (f32[2048]{0:T(1024)S(1)}, f32[2048]{0:T(1024)}, u32[]{:S(2)}) copy-start(f32[2048]{0:T(1024)} %param.20) | copy-start | bytes 24580
  46.0 77.7 %all-reduce.2.cloned.1.call-start = ((), (), s32[]{:S(2)}) async-start(), calls=%async_computation.6 | async-start | bytes 1048576 | tf_op jit(solution)/shard_map/psum | solution.py:106
  225.4 2.0 copy-start.2
  258.1 5.2 %copy-start.8 = (bf16[2048,64]{0,1:T(8,128)(2,1)S(1)}, bf16[2048,64]{0,1:T(8,128)(2,1)}, u32[]{:S(2)}) copy-start(bf16[2048,64]{0,1:T(8,128)(2,1)} %param.21) | copy-start | bytes 786436
  258.1 97.1 %all-to-all-start.2 = ((bf16[16,64,2048]{2,0,1:T(8,128)(2,1)}), bf16[16,64,2048]{2,0,1:T(8,128)(2,1)}, u32[]{:S(2)}, u32[]{:S(2)}) async-start(bf16[16,64,2048]{2,0,1:T(8,128)(2,1)} %copy.141), calls=%async_computation.2 | async-start | bytes 8388608 | tf_op jit(solution)/shard_map/all_to_all | solution.py:145
  262.8 105.7 %reduce-scatter.2.cloned.1.call-start = ((), (), s32[]{:S(2)}) async-start(), calls=%async_computation.7 | async-start | bytes 393216 | tf_op jit(solution)/shard_map/reduce_scatter | solution.py:149
  355.2 13.2 %copy-start.1 = (bf16[64,8,576]{2,1,0:T(8,128)(2,1)S(1)}, bf16[64,8,576]{2,1,0:T(8,128)(2,1)}, u32[]{:S(2)}) copy-start(bf16[64,8,576]{2,1,0:T(8,128)(2,1)} %param.13) | copy-start | bytes 1769476
Sparse Core Ops, SparseCore 0:
  9.5 12.4 all-gather.2
  46.1 41.4 all-gather.4
  106.0 17.6 all-reduce.1
  361.6 6.7 reduce-scatter.1
